TPU v7x, 32 devices: a whole 2x2x4 slice. The times are simulated.
32 devices in a mesh: ctx: 8 (over y, x, core), qry: 4 (over z).
Axes of the slice: x: 2, y: 2, z: 4, core: 2. Of those that a mesh axis runs over, the one named last changes fastest.
Arguments:
- hist_bins: int32 [512, 16], P(('ctx', 'qry')), may hold values from 0 to 63
- hist_ranks: int32 [512], P(('ctx', 'qry')), may hold values from 0 to 511, each once
- query_bins: int32 [32768, 16], P(('ctx', 'qry')), may hold values from 0 to 63
- bin_table: bfloat16 [1024, 512], replicated, may hold values from -4.5 to 4.5
- rank_vector: bfloat16 [512], replicated, may hold values from -5 to 5
- w_query: bfloat16 [512, 512], replicated, may hold values from -5.833631 to 5.833631
- w_key: bfloat16 [512, 512], replicated, may hold values from -0.176776695 to 0.176776695
- w_value: bfloat16 [512, 512], replicated, may hold values from -0.25 to 0.25
- w_out: bfloat16 [512, 512], replicated, may hold values from -0.25 to 0.25
- w_up: bfloat16 [512, 2048], replicated, may hold values from -0.25 to 0.25
- w_down: bfloat16 [2048, 512], replicated, may hold values from -0.125 to 0.125
Outputs:
- hist_out: bfloat16 [512, 512], P(('ctx', 'qry'))
- query_out: bfloat16 [32768, 512], P(('ctx', 'qry'))
All inputs are finite; a program needn't handle non-finite values.
Results may differ from a plain program's by a relative error of at most 0.008.
Values may be sent and summed in bfloat16 or wider, within the bound.
A program may use at most 64 MiB of HBM per device.

v0:
```python
import jax
import jax.numpy as jnp
from jax import lax
from jax.sharding import PartitionSpec as P

HEADS = 8
epsilon = 1e-05


def passed_along(block, axis, distance):
    devices = range(lax.axis_size(axis))
    route = [((i - distance) % len(devices), i) for i in devices]
    return lax.ppermute(block, axis, route)


def normalize(values):
    centered = values - jnp.mean(values, axis=-1, keepdims=True)
    variance = jnp.mean(centered * centered, axis=-1, keepdims=True)
    return centered * lax.rsqrt(variance + epsilon)


def embed_bins(bin_rows, bin_table):
    bin_count = bin_table.shape[0] // bin_rows.shape[1]
    columns = lax.broadcasted_iota(jnp.int32, (1, bin_count), 1)
    pieces = [
        (bin_rows[:, feature : feature + 1] == columns).astype(jnp.bfloat16)
        for feature in range(bin_rows.shape[1])
    ]
    one_hot = jnp.concatenate(pieces, axis=1)
    return jnp.dot(one_hot, bin_table, preferred_element_type=jnp.float32)


def history_rows(bin_rows, rank_ids, bin_table, rank_vector, history_total):
    level = (2.0 * rank_ids.astype(jnp.float32) + 1.0) / history_total - 1.0
    return (
        embed_bins(bin_rows, bin_table) + level[:, None] * rank_vector.astype(jnp.float32)[None, :]
    )


def pair_move(arrived, offset):
    return passed_along(arrived, "ctx", offset)


def circulate_one(first_block, carry_state, absorb, mover, group_count):

    def advance(step_index, loop_carry):
        moving, current = loop_carry
        moving = mover(moving, 1)
        return (moving, absorb(current, moving))

    return lax.fori_loop(0, group_count - 1, advance, (first_block, carry_state))[1]


def local(
    hist_bins,
    hist_ranks,
    query_bins,
    bin_table,
    rank_vector,
    w_query,
    w_key,
    w_value,
    w_out,
    w_up,
    w_down,
):
    group_count = lax.axis_size("ctx")
    own_rows = hist_bins.shape[0]
    history_total = float(own_rows * group_count * lax.axis_size("qry"))
    own_embed = history_rows(hist_bins, hist_ranks, bin_table, rank_vector, history_total)
    all_rows = jnp.concatenate([own_embed, embed_bins(query_bins, bin_table)], axis=0)
    normed = normalize(all_rows).astype(jnp.bfloat16)
    queries = jnp.dot(normed, w_query, preferred_element_type=jnp.float32).astype(jnp.bfloat16)
    row_count = all_rows.shape[0]
    head_dim = w_query.shape[1] // HEADS
    scale = head_dim ** (-0.5)
    query_heads = queries.reshape(row_count, HEADS, head_dim)
    initial = (
        jnp.full((HEADS, row_count), -1e30, jnp.float32),
        jnp.zeros((HEADS, row_count), jnp.float32),
        jnp.zeros((HEADS, row_count, head_dim), jnp.float32),
    )

    def absorb_pair(carry_state, key_rows, value_rows):
        row_peak, row_total, summed = carry_state
        key_heads = key_rows.reshape(-1, HEADS, head_dim)
        value_heads = value_rows.reshape(-1, HEADS, head_dim)
        scores = (
            jnp.einsum("nhd,khd->hnk", query_heads, key_heads, preferred_element_type=jnp.float32)
            * scale
        )
        new_peak = jnp.maximum(row_peak, jnp.max(scores, axis=-1))
        factor = jnp.exp(row_peak - new_peak)
        weights = jnp.exp(scores - new_peak[..., None])
        row_total = row_total * factor + jnp.sum(weights, axis=-1)
        summed = summed * factor[..., None] + jnp.einsum(
            "hnk,khd->hnd",
            weights.astype(jnp.bfloat16),
            value_heads,
            preferred_element_type=jnp.float32,
        )
        return (new_peak, row_total, summed)

    history_normed = normed[:own_rows]
    key_rows = jnp.dot(history_normed, w_key, preferred_element_type=jnp.float32).astype(
        jnp.bfloat16
    )
    value_rows = jnp.dot(history_normed, w_value, preferred_element_type=jnp.float32).astype(
        jnp.bfloat16
    )
    key_pairs = jnp.stack((key_rows, value_rows))
    first_block = lax.all_gather(key_pairs, "qry", axis=1, tiled=True)

    def absorb(carry_state, arrived):
        return absorb_pair(carry_state, arrived[0], arrived[1])

    carry_state = absorb(initial, first_block)
    carry_state = circulate_one(first_block, carry_state, absorb, pair_move, group_count)
    row_peak, row_total, summed = carry_state
    attended = (
        jnp.transpose(summed / row_total[..., None], (1, 0, 2))
        .reshape(row_count, -1)
        .astype(jnp.bfloat16)
    )
    after_attention = all_rows + jnp.dot(attended, w_out, preferred_element_type=jnp.float32)
    inner = jnp.dot(
        normalize(after_attention).astype(jnp.bfloat16), w_up, preferred_element_type=jnp.float32
    )
    hidden = jax.nn.gelu(inner, approximate=True).astype(jnp.bfloat16)
    result = (after_attention + jnp.dot(hidden, w_down, preferred_element_type=jnp.float32)).astype(
        jnp.bfloat16
    )
    return (result[:own_rows], result[own_rows:])


def solution(mesh):
    return jax.shard_map(
        local,
        mesh=mesh,
        in_specs=(
            P(("ctx", "qry"), None),
            P(("ctx", "qry")),
            P(("ctx", "qry"), None),
            P(),
            P(),
            P(),
            P(),
            P(),
            P(),
            P(),
            P(),
        ),
        out_specs=(P(("ctx", "qry"), None), P(("ctx", "qry"), None)),
        check_vma=False,
    )
```

profile of v0, /device:TPU:0, one launch (start us, length us, event | category | flops | bytes accessed | tf_op | source)
XLA Modules:
  0.0 152.9 jit_solution(12912885577135275044)
XLA Ops:
  2.1 1.7 %slice_reduce_fusion = (s32[16]{0:T(128)S(1)}, s32[16]{0:T(128)S(1)}, s32[16]{0:T(128)S(1)}, s32[16]{0:T(128)S(1)}, s32[16]{0:T(128)S(1)}, /*index=5*/s32[16]{0:...) fusion(s32[16,16]{1,0:T(8,128)} %param.13), kind=kLoop, calls=%fused_computation.67 | loop fusion | bytes 2048 | tf_op jit(solution)/shard_map/slice | solution.py:26
  4.6 1.5 convolution_add_fusion.4
  6.1 1.3 fusion.36
  15.0 5.7 %concatenate.17 = pred[1024,1024]{1,0:T(32,128)(4,1)S(1)} concatenate(pred[1024,64]{1,0:T(32,128)(4,1)} %get-tuple-element.116, pred[1024,64]{1,0:T(32,128)(4,1)} %get-tuple-element.115, pred[1024,64]{1,0:T(32,128)(4,1)} %get-tuple-element.114, pred[1024,64]{1,0:T(32,128)(4,1)} %get-tuple-element.113, pred[1024,64]{1,0:T(32,128)(4,1)} %get-tuple-element.112, ...), dimensions={1} | concatenate | bytes 2097152 | tf_op jit(solution)/shard_map/concatenate | solution.py:29
  20.7 2.5 %fusion.39 = f32[1024,512]{1,0:T(8,128)S(1)} fusion(pred[1024,1024]{1,0:T(32,128)(4,1)S(1)} %concatenate.17, bf16[1024,512]{1,0:T(8,128)(2,1)} %param.16), kind=kOutput, calls=%fused_computation.112 | convolution fusion | flops 1073741824 | bytes 4194304 | tf_op jit(solution)/shard_map/dot_general | solution.py:30
  25.6 1.7 %convolution_convert_fusion = bf16[1040,512]{1,0:T(8,128)(2,1)} fusion(bf16[1040,512]{1,0:T(8,128)(2,1)S(1)} %multiply_convert_fusion.1, bf16[512,512]{1,0:T(8,128)(2,1)S(1)} %copy-done.19), kind=kOutput, calls=%fused_computation.23 | convolution fusion | flops 545792000 | bytes 2654208 | tf_op jit(solution)/shard_map/dot_general | solution.py:73
  27.3 15.2 %all_gather.3 = bf16[2,64,512]{2,1,0:T(8,128)(2,1)S(1)} all-gather(bf16[2,16,512]{2,1,0:T(8,128)(2,1)S(1)} %pad_maximum_fusion.1), channel_id=1, replica_groups=mesh['ctx'=8,'qry'=4] {'qry'}, dimensions={1}, use_global_device_ids=true | all-gather | bytes 163840 | tf_op jit(solution)/shard_map/all_gather | solution.py:112
  42.5 1.7 %copy.20 = bf16[1040,512]{0,1:T(8,128)(2,1)S(1)} copy(bf16[1040,512]{1,0:T(8,128)(2,1)} %convolution_convert_fusion) | data formatting | bytes 2129920 | tf_op jit(solution)/shard_map/convert_element_type | solution.py:73
  47.5 1.9 %convolution_add_fusion.2 = f32[8,1040,64]{1,2,0:T(8,128)} fusion(bf16[64,8,64]{0,2,1:T(8,128)(2,1)S(1)} %bitcast.52, f32[8,1040,64]{1,2,0:T(8,128)S(1)} %get-tuple-element.98, f32[8,1040]{1,0:T(8,128)S(1)} %get-tuple-element.95, f32[8,1040]{1,0:T(8,128)S(1)} %broadcast_maximum_fusion), kind=kOutput, calls=%fused_computation.19 | convolution fusion | flops 69754880 | bytes 4391936 | tf_op jit(solution)/shard_map/hnk,khd->hnd/dot_general | solution.py:96
  49.4 88.3 %while.16 = (s32[]{:T(128)}, bf16[2,64,512]{2,1,0:T(8,128)(2,1)S(1)}, f32[8,1040]{1,0:T(8,128)}, f32[8,1040]{1,0:T(8,128)}, f32[8,1040,64]{1,2,0:T(8,128)}, /*index=5*/bf16[1040,8,64]{0,2,1:T(8,128)(2,1)S(1)}, s32[]{:T(128)}) while((s32[]{:T(128)}, bf16[2,64,512]{2,1,0:T(8,128)(2,1)S(1)}, f32[8,1040]{1,0:T(8,128)}, f32[8,1040]{1,0:T(8,128)}, ...), condition=%wide.region_7.0_spmd, body=%wide.region_4.0_spmd.sunk | while | flops 140591360 | bytes 32176440 | solution.py:51
  49.4 5.3 %collective-permute-done = bf16[2,64,512]{2,1,0:T(8,128)(2,1)S(1)} collective-permute-done((bf16[2,64,512]{2,1,0:T(8,128)(2,1)S(1)}, bf16[2,64,512]{2,1,0:T(8,128)(2,1)S(1)}, u32[]{:S(2)}, u32[]{:S(2)}) %collective-permute-start) | collective-permute-done | bytes 131104 | tf_op jit(solution)/shard_map/while/body/eval_jaxpr/ppermute | solution.py:13
  59.6 1.1 convolution_add_fusion.6
  60.7 1.4 copy-done.2
  62.1 5.3 %collective-permute-done = bf16[2,64,512]{2,1,0:T(8,128)(2,1)S(1)} collective-permute-done((bf16[2,64,512]{2,1,0:T(8,128)(2,1)S(1)}, bf16[2,64,512]{2,1,0:T(8,128)(2,1)S(1)}, u32[]{:S(2)}, u32[]{:S(2)}) %collective-permute-start) | collective-permute-done | bytes 131104 | tf_op jit(solution)/shard_map/while/body/eval_jaxpr/ppermute | solution.py:13
  72.2 1.1 convolution_add_fusion.6
  73.3 1.4 copy-done.2
  74.7 5.3 %collective-permute-done = bf16[2,64,512]{2,1,0:T(8,128)(2,1)S(1)} collective-permute-done((bf16[2,64,512]{2,1,0:T(8,128)(2,1)S(1)}, bf16[2,64,512]{2,1,0:T(8,128)(2,1)S(1)}, u32[]{:S(2)}, u32[]{:S(2)}) %collective-permute-start) | collective-permute-done | bytes 131104 | tf_op jit(solution)/shard_map/while/body/eval_jaxpr/ppermute | solution.py:13
  84.8 1.1 convolution_add_fusion.6
  85.9 1.4 copy-done.2
  87.3 5.3 %collective-permute-done = bf16[2,64,512]{2,1,0:T(8,128)(2,1)S(1)} collective-permute-done((bf16[2,64,512]{2,1,0:T(8,128)(2,1)S(1)}, bf16[2,64,512]{2,1,0:T(8,128)(2,1)S(1)}, u32[]{:S(2)}, u32[]{:S(2)}) %collective-permute-start) | collective-permute-done | bytes 131104 | tf_op jit(solution)/shard_map/while/body/eval_jaxpr/ppermute | solution.py:13
  97.4 1.1 convolution_add_fusion.6
  98.5 1.4 copy-done.2
  99.9 5.3 %collective-permute-done = bf16[2,64,512]{2,1,0:T(8,128)(2,1)S(1)} collective-permute-done((bf16[2,64,512]{2,1,0:T(8,128)(2,1)S(1)}, bf16[2,64,512]{2,1,0:T(8,128)(2,1)S(1)}, u32[]{:S(2)}, u32[]{:S(2)}) %collective-permute-start) | collective-permute-done | bytes 131104 | tf_op jit(solution)/shard_map/while/body/eval_jaxpr/ppermute | solution.py:13
  111.1 1.4 copy-done.2
  112.5 5.3 %collective-permute-done = bf16[2,64,512]{2,1,0:T(8,128)(2,1)S(1)} collective-permute-done((bf16[2,64,512]{2,1,0:T(8,128)(2,1)S(1)}, bf16[2,64,512]{2,1,0:T(8,128)(2,1)S(1)}, u32[]{:S(2)}, u32[]{:S(2)}) %collective-permute-start) | collective-permute-done | bytes 131104 | tf_op jit(solution)/shard_map/while/body/eval_jaxpr/ppermute | solution.py:13
  122.6 1.1 convolution_add_fusion.6
  123.7 1.4 copy-done.2
  125.1 5.3 %collective-permute-done = bf16[2,64,512]{2,1,0:T(8,128)(2,1)S(1)} collective-permute-done((bf16[2,64,512]{2,1,0:T(8,128)(2,1)S(1)}, bf16[2,64,512]{2,1,0:T(8,128)(2,1)S(1)}, u32[]{:S(2)}, u32[]{:S(2)}) %collective-permute-start) | collective-permute-done | bytes 131104 | tf_op jit(solution)/shard_map/while/body/eval_jaxpr/ppermute | solution.py:13
  136.3 1.4 copy-done.2
  137.7 2.0 %divide_convert_fusion = bf16[8,1040,64]{1,2,0:T(8,128)(2,1)S(1)} fusion(f32[8,1040,64]{1,2,0:T(8,128)} %get-tuple-element.35, f32[8,1040]{1,0:T(8,128)} %get-tuple-element.36), kind=kLoop, calls=%fused_computation.24 | loop fusion | flops 1064960 | bytes 3228160 | tf_op jit(solution)/shard_map/convert_element_type | solution.py:123
  141.0 1.3 copy-done.7
  142.8 8.4 %fusion.13 = bf16[1040,512]{1,0:T(8,128)(2,1)S(1)} fusion(f32[1040,512]{1,0:T(8,128)} %copy-done.7, bf16[2048,512]{1,0:T(8,128)(2,1)S(1)} %copy-done, bf16[512,2048]{1,0:T(8,128)(2,1)} %param.22, f32[1040]{0:T(1024)S(1)} %add_rsqrt_fusion, f32[1040]{0:T(1024)S(1)} %broadcast_multiply_fusion), kind=kOutput, calls=%fused_computation.22 | convolution fusion | flops 4383907840 | bytes 7397504 | tf_op jit(solution)/shard_map/dot_general | solution.py:130
  (228 shorter events, 54.3 us)
Async XLA Ops:
  0.6 142.2 %copy-start = (bf16[2048,512]{1,0:T(8,128)(2,1)S(1)}, bf16[2048,512]{1,0:T(8,128)(2,1)}, u32[]{:S(2)}) copy-start(bf16[2048,512]{1,0:T(8,128)(2,1)} %param.23) | copy-start | bytes 6291460
  6.1 17.9 %copy-start.12 = (f32[16,512]{1,0:T(8,128)}, f32[16,512]{1,0:T(8,128)S(1)}, u32[]{:S(2)}) copy-start(f32[16,512]{1,0:T(8,128)S(1)} %convolution_add_fusion.4) | copy-start | bytes 98308
  42.5 2.3 %copy-start.15 = (bf16[2,64,512]{2,1,0:T(8,128)(2,1)}, bf16[2,64,512]{2,1,0:T(8,128)(2,1)S(1)}, u32[]{:S(2)}) copy-start(bf16[2,64,512]{2,1,0:T(8,128)(2,1)S(1)} %all_gather.3) | copy-start | bytes 393220
  46.5 3.0 %copy-start.8 = (f32[8,1040]{1,0:T(8,128)}, f32[8,1040]{1,0:T(8,128)S(1)}, u32[]{:S(2)}) copy-start(f32[8,1040]{1,0:T(8,128)S(1)} %broadcast_maximum_fusion) | copy-start | bytes 99844
  47.5 1.9 %copy-start.16 = (bf16[2,64,512]{2,1,0:T(8,128)(2,1)S(1)}, bf16[2,64,512]{2,1,0:T(8,128)(2,1)}, u32[]{:S(2)}) copy-start(bf16[2,64,512]{2,1,0:T(8,128)(2,1)} %copy-done.15) | copy-start | bytes 393220
  49.4 5.3 %collective-permute-start = (bf16[2,64,512]{2,1,0:T(8,128)(2,1)S(1)}, bf16[2,64,512]{2,1,0:T(8,128)(2,1)S(1)}, u32[]{:S(2)}, u32[]{:S(2)}) collective-permute-start(bf16[2,64,512]{2,1,0:T(8,128)(2,1)S(1)} %get-tuple-element.190), channel_id=1, source_target_pairs={{28,0},{0,4},{4,8},{8,12},{12,16},{16,20},{20,24},{24,28},{29,1},{... | collective-permute-start | bytes 393224 | tf_op jit(solution)/shard_map/while/body/eval_jaxpr/ppermute | solution.py:13
  54.7 1.7 %copy-start.5 = (bf16[2,64,512]{2,1,0:T(8,128)(2,1)}, bf16[2,64,512]{2,1,0:T(8,128)(2,1)S(1)}, u32[]{:S(2)}) copy-start(bf16[2,64,512]{2,1,0:T(8,128)(2,1)S(1)} %collective-permute-done) | copy-start | bytes 393220 | tf_op jit(solution)/shard_map/while
  57.9 1.7 %copy-start.1 = (f32[8,1040,64]{1,2,0:T(8,128)S(1)}, f32[8,1040,64]{1,2,0:T(8,128)}, u32[]{:S(2)}) copy-start(f32[8,1040,64]{1,2,0:T(8,128)} %get-tuple-element.193) | copy-start | bytes 6389764 | tf_op jit(solution)/shard_map/while
  58.7 2.0 %copy-start.11 = (f32[8,1040]{1,0:T(8,128)}, f32[8,1040]{1,0:T(8,128)S(1)}, u32[]{:S(2)}) copy-start(f32[8,1040]{1,0:T(8,128)S(1)} %get-tuple-element.199) | copy-start | bytes 99844 | tf_op jit(solution)/shard_map/while
  62.1 5.3 %collective-permute-start = (bf16[2,64,512]{2,1,0:T(8,128)(2,1)S(1)}, bf16[2,64,512]{2,1,0:T(8,128)(2,1)S(1)}, u32[]{:S(2)}, u32[]{:S(2)}) collective-permute-start(bf16[2,64,512]{2,1,0:T(8,128)(2,1)S(1)} %get-tuple-element.190), channel_id=1, source_target_pairs={{28,0},{0,4},{4,8},{8,12},{12,16},{16,20},{20,24},{24,28},{29,1},{... | collective-permute-start | bytes 393224 | tf_op jit(solution)/shard_map/while/body/eval_jaxpr/ppermute | solution.py:13
  67.4 1.7 %copy-start.5 = (bf16[2,64,512]{2,1,0:T(8,128)(2,1)}, bf16[2,64,512]{2,1,0:T(8,128)(2,1)S(1)}, u32[]{:S(2)}) copy-start(bf16[2,64,512]{2,1,0:T(8,128)(2,1)S(1)} %collective-permute-done) | copy-start | bytes 393220 | tf_op jit(solution)/shard_map/while
  70.5 1.7 %copy-start.1 = (f32[8,1040,64]{1,2,0:T(8,128)S(1)}, f32[8,1040,64]{1,2,0:T(8,128)}, u32[]{:S(2)}) copy-start(f32[8,1040,64]{1,2,0:T(8,128)} %get-tuple-element.193) | copy-start | bytes 6389764 | tf_op jit(solution)/shard_map/while
  71.3 2.0 %copy-start.11 = (f32[8,1040]{1,0:T(8,128)}, f32[8,1040]{1,0:T(8,128)S(1)}, u32[]{:S(2)}) copy-start(f32[8,1040]{1,0:T(8,128)S(1)} %get-tuple-element.199) | copy-start | bytes 99844 | tf_op jit(solution)/shard_map/while
  74.7 5.3 %collective-permute-start = (bf16[2,64,512]{2,1,0:T(8,128)(2,1)S(1)}, bf16[2,64,512]{2,1,0:T(8,128)(2,1)S(1)}, u32[]{:S(2)}, u32[]{:S(2)}) collective-permute-start(bf16[2,64,512]{2,1,0:T(8,128)(2,1)S(1)} %get-tuple-element.190), channel_id=1, source_target_pairs={{28,0},{0,4},{4,8},{8,12},{12,16},{16,20},{20,24},{24,28},{29,1},{... | collective-permute-start | bytes 393224 | tf_op jit(solution)/shard_map/while/body/eval_jaxpr/ppermute | solution.py:13
  83.1 1.7 %copy-start.1 = (f32[8,1040,64]{1,2,0:T(8,128)S(1)}, f32[8,1040,64]{1,2,0:T(8,128)}, u32[]{:S(2)}) copy-start(f32[8,1040,64]{1,2,0:T(8,128)} %get-tuple-element.193) | copy-start | bytes 6389764 | tf_op jit(solution)/shard_map/while
  83.9 2.0 %copy-start.11 = (f32[8,1040]{1,0:T(8,128)}, f32[8,1040]{1,0:T(8,128)S(1)}, u32[]{:S(2)}) copy-start(f32[8,1040]{1,0:T(8,128)S(1)} %get-tuple-element.199) | copy-start | bytes 99844 | tf_op jit(solution)/shard_map/while
  87.3 5.3 %collective-permute-start = (bf16[2,64,512]{2,1,0:T(8,128)(2,1)S(1)}, bf16[2,64,512]{2,1,0:T(8,128)(2,1)S(1)}, u32[]{:S(2)}, u32[]{:S(2)}) collective-permute-start(bf16[2,64,512]{2,1,0:T(8,128)(2,1)S(1)} %get-tuple-element.190), channel_id=1, source_target_pairs={{28,0},{0,4},{4,8},{8,12},{12,16},{16,20},{20,24},{24,28},{29,1},{... | collective-permute-start | bytes 393224 | tf_op jit(solution)/shard_map/while/body/eval_jaxpr/ppermute | solution.py:13
  92.6 1.7 %copy-start.5 = (bf16[2,64,512]{2,1,0:T(8,128)(2,1)}, bf16[2,64,512]{2,1,0:T(8,128)(2,1)S(1)}, u32[]{:S(2)}) copy-start(bf16[2,64,512]{2,1,0:T(8,128)(2,1)S(1)} %collective-permute-done) | copy-start | bytes 393220 | tf_op jit(solution)/shard_map/while
  95.7 1.7 %copy-start.1 = (f32[8,1040,64]{1,2,0:T(8,128)S(1)}, f32[8,1040,64]{1,2,0:T(8,128)}, u32[]{:S(2)}) copy-start(f32[8,1040,64]{1,2,0:T(8,128)} %get-tuple-element.193) | copy-start | bytes 6389764 | tf_op jit(solution)/shard_map/while
  96.5 2.0 %copy-start.11 = (f32[8,1040]{1,0:T(8,128)}, f32[8,1040]{1,0:T(8,128)S(1)}, u32[]{:S(2)}) copy-start(f32[8,1040]{1,0:T(8,128)S(1)} %get-tuple-element.199) | copy-start | bytes 99844 | tf_op jit(solution)/shard_map/while
  99.9 5.3 %collective-permute-start = (bf16[2,64,512]{2,1,0:T(8,128)(2,1)S(1)}, bf16[2,64,512]{2,1,0:T(8,128)(2,1)S(1)}, u32[]{:S(2)}, u32[]{:S(2)}) collective-permute-start(bf16[2,64,512]{2,1,0:T(8,128)(2,1)S(1)} %get-tuple-element.190), channel_id=1, source_target_pairs={{28,0},{0,4},{4,8},{8,12},{12,16},{16,20},{20,24},{24,28},{29,1},{... | collective-permute-start | bytes 393224 | tf_op jit(solution)/shard_map/while/body/eval_jaxpr/ppermute | solution.py:13
  108.3 1.7 %copy-start.1 = (f32[8,1040,64]{1,2,0:T(8,128)S(1)}, f32[8,1040,64]{1,2,0:T(8,128)}, u32[]{:S(2)}) copy-start(f32[8,1040,64]{1,2,0:T(8,128)} %get-tuple-element.193) | copy-start | bytes 6389764 | tf_op jit(solution)/shard_map/while
  109.1 2.0 %copy-start.11 = (f32[8,1040]{1,0:T(8,128)}, f32[8,1040]{1,0:T(8,128)S(1)}, u32[]{:S(2)}) copy-start(f32[8,1040]{1,0:T(8,128)S(1)} %get-tuple-element.199) | copy-start | bytes 99844 | tf_op jit(solution)/shard_map/while
  112.5 5.3 %collective-permute-start = (bf16[2,64,512]{2,1,0:T(8,128)(2,1)S(1)}, bf16[2,64,512]{2,1,0:T(8,128)(2,1)S(1)}, u32[]{:S(2)}, u32[]{:S(2)}) collective-permute-start(bf16[2,64,512]{2,1,0:T(8,128)(2,1)S(1)} %get-tuple-element.190), channel_id=1, source_target_pairs={{28,0},{0,4},{4,8},{8,12},{12,16},{16,20},{20,24},{24,28},{29,1},{... | collective-permute-start | bytes 393224 | tf_op jit(solution)/shard_map/while/body/eval_jaxpr/ppermute | solution.py:13
  120.9 1.7 %copy-start.1 = (f32[8,1040,64]{1,2,0:T(8,128)S(1)}, f32[8,1040,64]{1,2,0:T(8,128)}, u32[]{:S(2)}) copy-start(f32[8,1040,64]{1,2,0:T(8,128)} %get-tuple-element.193) | copy-start | bytes 6389764 | tf_op jit(solution)/shard_map/while
  121.7 2.0 %copy-start.11 = (f32[8,1040]{1,0:T(8,128)}, f32[8,1040]{1,0:T(8,128)S(1)}, u32[]{:S(2)}) copy-start(f32[8,1040]{1,0:T(8,128)S(1)} %get-tuple-element.199) | copy-start | bytes 99844 | tf_op jit(solution)/shard_map/while
  125.1 5.3 %collective-permute-start = (bf16[2,64,512]{2,1,0:T(8,128)(2,1)S(1)}, bf16[2,64,512]{2,1,0:T(8,128)(2,1)S(1)}, u32[]{:S(2)}, u32[]{:S(2)}) collective-permute-start(bf16[2,64,512]{2,1,0:T(8,128)(2,1)S(1)} %get-tuple-element.190), channel_id=1, source_target_pairs={{28,0},{0,4},{4,8},{8,12},{12,16},{16,20},{20,24},{24,28},{29,1},{... | collective-permute-start | bytes 393224 | tf_op jit(solution)/shard_map/while/body/eval_jaxpr/ppermute | solution.py:13
  133.5 1.7 %copy-start.1 = (f32[8,1040,64]{1,2,0:T(8,128)S(1)}, f32[8,1040,64]{1,2,0:T(8,128)}, u32[]{:S(2)}) copy-start(f32[8,1040,64]{1,2,0:T(8,128)} %get-tuple-element.193) | copy-start | bytes 6389764 | tf_op jit(solution)/shard_map/while
  134.3 2.0 %copy-start.11 = (f32[8,1040]{1,0:T(8,128)}, f32[8,1040]{1,0:T(8,128)S(1)}, u32[]{:S(2)}) copy-start(f32[8,1040]{1,0:T(8,128)S(1)} %get-tuple-element.199) | copy-start | bytes 99844 | tf_op jit(solution)/shard_map/while
  137.7 2.3 %copy-start.4 = (f32[1024,512]{1,0:T(8,128)S(1)}, f32[1024,512]{1,0:T(8,128)}, u32[]{:S(2)}) copy-start(f32[1024,512]{1,0:T(8,128)} %copy-done.3) | copy-start | bytes 6291460
  137.7 2.3 %copy-start.13 = (f32[16,512]{1,0:T(8,128)S(1)}, f32[16,512]{1,0:T(8,128)}, u32[]{:S(2)}) copy-start(f32[16,512]{1,0:T(8,128)} %copy-done.12) | copy-start | bytes 98308
  137.7 2.4 %copy-start.14 = (bf16[512,512]{1,0:T(8,128)(2,1)S(1)}, bf16[512,512]{1,0:T(8,128)(2,1)}, u32[]{:S(2)}) copy-start(bf16[512,512]{1,0:T(8,128)(2,1)} %param.21) | copy-start | bytes 1572868
  (37 other events, 41.1 us)
where the time goes:
time: 155 us; the launch traced here: 153 us
  local copies, waits for them, and re-layouts  53.6 us (35%)
  waiting for transfers between devices  37 us (24%)
  matrix products  28.3 us (18%)
  other arithmetic  17.1 us (11%)
  blocking collectives  15.2 us (10%)
    ppermute x7, waiting for transfers between devices, passed_along(): return lax.ppermute(block, axis, route)  37 us
    while x112, local copies, waits for them, and re-layouts  18.7 us
    all_gather x1, blocking collectives, local(): first_block = lax.all_gather(key_pairs, 'qry', axis=1, tiled=True)  15.2 us
    slice x15, local copies, waits for them, and re-layouts, absorb(): return absorb_pair(carry_state, arrived[0], arrived[1])  12.1 us
    dot_general x8, matrix products, absorb_pair(): jnp.einsum('hnk,khd->hnd', weights.astype(jnp.bfloat16), value_heads, pre...  9.39 us
    dot_general x1, matrix products, local(): jnp.dot(hidden, w_down, preferred_element_type=jnp.float32)  8.4 us
    eq x16, other arithmetic, embed_bins(): bin_rows[:, feature:feature + 1] == columns  8.22 us
    squeeze x7, local copies, waits for them, and re-layouts, absorb_pair(): key_heads = key_rows.reshape(-1, HEADS, head_dim)  6.83 us
  transfers between devices with their start and end apart: 7, of which 7 were waited for; matrix products, arithmetic and copies ran while one was open for 0% of the time, Pallas kernels for 0%

commit v1 on v0

--- a/solution.py
+++ b/solution.py
@@ -1,3 +1,4 @@
+import functools
 import jax
 import jax.numpy as jnp
 from jax import lax
@@ -5,6 +6,16 @@
 
 HEADS = 8
 epsilon = 1e-05
+
+
+def _switch_sources_all(page, peer_axis):
+    b_next = tuple((page for _ in range(jax.lax.psum(1, peer_axis))))
+    spare = jnp.stack(b_next)
+    clean = jax.lax.all_to_all(spare, peer_axis, 0, 0)
+    return jnp.concatenate(clean, axis=1)
+
+
+take_outputs = functools.partial(_switch_sources_all, peer_axis="qry")
 
 
 def passed_along(block, axis, distance):
@@ -109,7 +120,7 @@
         jnp.bfloat16
     )
     key_pairs = jnp.stack((key_rows, value_rows))
-    first_block = lax.all_gather(key_pairs, "qry", axis=1, tiled=True)
+    first_block = take_outputs(key_pairs)
 
     def absorb(carry_state, arrived):
         return absorb_pair(carry_state, arrived[0], arrived[1])

time: 155 us -> 157 us (1.013)
  blocking collectives: 15.2 us -> 0 us
  starting transfers between devices: 0.02 us -> 6.34 us
  other arithmetic: 17.1 us -> 23.3 us
  matrix products: 28.3 us -> 30.9 us
  waiting for transfers between devices: 37 us -> 38.7 us
    all_gather x1 -> x0, blocking collectives: 15.2 us -> none  [local(): first_block = lax.all_gather(key_pairs, 'qry', axis=1, tiled=True)]
    all_to_all x0 -> x1, starting transfers between devices: none -> 6.32 us  [_switch_sources_all(): clean = jax.lax.all_to_all(spare, peer_axis, 0, 0)]
    eq x16, other arithmetic: 8.22 us -> 12.3 us  [embed_bins(): bin_rows[:, feature:feature + 1] == columns]
    all_to_all x0 -> x1, waiting for transfers between devices: none -> 1.66 us  [_switch_sources_all(): clean = jax.lax.all_to_all(spare, peer_axis, 0, 0)]
    reduce_sum x1, other arithmetic: 0.25 us -> 1.86 us  [normalize(): centered = values - jnp.mean(values, axis=-1, keepdims=True)]
  transfers between devices with their start and end apart: 7 -> 8, of which waited for: 7 -> 8; matrix products, arithmetic and copies ran while one was open for 0% -> 3% of each run, Pallas kernels for 0% -> 0%
where the time goes in v1:
time: 157 us; the launch traced here: 155 us
  local copies, waits for them, and re-layouts  53.9 us (34%)
  waiting for transfers between devices  38.7 us (25%)
  matrix products  30.9 us (20%)
  other arithmetic  23.3 us (15%)
  starting transfers between devices  6.34 us (4%)
    ppermute x7, waiting for transfers between devices, passed_along(): return lax.ppermute(block, axis, route)  37 us
    while x112, local copies, waits for them, and re-layouts  18.7 us
    eq x16, other arithmetic, embed_bins(): bin_rows[:, feature:feature + 1] == columns  12.3 us
    slice x15, local copies, waits for them, and re-layouts, absorb(): return absorb_pair(carry_state, arrived[0], arrived[1])  12.1 us
    dot_general x8, matrix products, absorb_pair(): jnp.einsum('hnk,khd->hnd', weights.astype(jnp.bfloat16), value_heads, pre...  9.47 us
    dot_general x1, matrix products, local(): jnp.dot(hidden, w_down, preferred_element_type=jnp.float32)  8.39 us
    squeeze x7, local copies, waits for them, and re-layouts, absorb_pair(): key_heads = key_rows.reshape(-1, HEADS, head_dim)  6.83 us
    all_to_all x1, starting transfers between devices, _switch_sources_all(): clean = jax.lax.all_to_all(spare, peer_axis, 0, 0)  6.32 us
  transfers between devices with their start and end apart: 8, of which 8 were waited for; matrix products, arithmetic and copies ran while one was open for 3% of the time, Pallas kernels for 0%

profile of v1, /device:TPU:0, one launch (start us, length us, event | category | flops | bytes accessed | tf_op | source)
XLA Modules:
  0.0 154.9 jit_solution(14770151080928655582)
XLA Ops:
  0.6 1.3 multiply_add_fusion.1
  2.7 1.7 %slice_reduce_fusion = (s32[16]{0:T(128)S(1)}, s32[16]{0:T(128)S(1)}, s32[16]{0:T(128)S(1)}, s32[16]{0:T(128)S(1)}, s32[16]{0:T(128)S(1)}, /*index=5*/s32[16]{0:...) fusion(s32[16,16]{1,0:T(8,128)} %param.13), kind=kLoop, calls=%fused_computation.68 | loop fusion | bytes 2048 | tf_op jit(solution)/shard_map/slice | solution.py:37
  4.4 1.3 fusion.37
  18.0 5.6 %concatenate.17 = pred[1024,1024]{1,0:T(32,128)(4,1)S(1)} concatenate(pred[1024,64]{1,0:T(32,128)(4,1)} %get-tuple-element.118, pred[1024,64]{1,0:T(32,128)(4,1)} %get-tuple-element.117, pred[1024,64]{1,0:T(32,128)(4,1)} %get-tuple-element.116, pred[1024,64]{1,0:T(32,128)(4,1)} %get-tuple-element.115, pred[1024,64]{1,0:T(32,128)(4,1)} %get-tuple-element.114, ...), dimensions={1} | concatenate | bytes 2097152 | tf_op jit(solution)/shard_map/concatenate | solution.py:40
  23.7 3.8 %fusion.40 = f32[1024,512]{1,0:T(8,128)} fusion(pred[1024,1024]{1,0:T(32,128)(4,1)S(1)} %concatenate.17, bf16[1024,512]{1,0:T(8,128)(2,1)} %param.16), kind=kOutput, calls=%fused_computation.114 | convolution fusion | flops 1073741824 | bytes 4194304 | tf_op jit(solution)/shard_map/dot_general | solution.py:41
  27.8 1.6 %convolution_add_fusion.4 = f32[16,512]{1,0:T(8,128)S(1)} fusion(pred[16,1024]{1,0:T(8,128)(4,1)S(1)} %concatenate.15, bf16[1024,512]{1,0:T(8,128)(2,1)} %param.16, f32[512]{0:T(512)S(1)} %convert_element_type.31, f32[16]{0:T(128)S(1)} %copy-done.32), kind=kOutput, calls=%fused_computation.34 | convolution fusion | flops 16793600 | bytes 1099840 | tf_op jit(solution)/shard_map/dot_general | solution.py:41
  29.4 1.9 %fusion.24 = f32[1040]{0:T(1024)S(1)} fusion(f32[1024,512]{1,0:T(8,128)} %fusion.40, f32[16,512]{1,0:T(8,128)S(1)} %convolution_add_fusion.4), kind=kLoop, calls=%fused_computation.41 | loop fusion | flops 1063920 | bytes 2134080 | tf_op jit(solution)/shard_map/reduce_sum | solution.py:28
  33.8 6.3 %all-to-all-start = ((bf16[4,2,16,512]{3,2,1,0:T(8,128)(2,1)}), bf16[4,2,16,512]{3,2,1,0:T(8,128)(2,1)S(1)}, u32[]{:S(2)}, u32[]{:S(2)}) async-start(bf16[4,2,16,512]{3,2,1,0:T(8,128)(2,1)} %stack.19), calls=%async_computation | async-start | bytes 262144 | tf_op jit(solution)/shard_map/all_to_all | solution.py:14
  40.1 2.7 %convolution_convert_fusion = bf16[1040,512]{1,0:T(8,128)(2,1)} fusion(bf16[1040,512]{1,0:T(8,128)(2,1)S(1)} %multiply_convert_fusion.1, bf16[512,512]{1,0:T(8,128)(2,1)} %param.18), kind=kOutput, calls=%fused_computation.23 | convolution fusion | flops 545792000 | bytes 2654208 | tf_op jit(solution)/shard_map/dot_general | solution.py:84
  42.9 1.7 %copy.24 = bf16[1040,512]{0,1:T(8,128)(2,1)S(1)} copy(bf16[1040,512]{1,0:T(8,128)(2,1)} %convolution_convert_fusion) | data formatting | bytes 2129920 | tf_op jit(solution)/shard_map/convert_element_type | solution.py:84
  44.5 1.7 %all-to-all-done = bf16[4,2,16,512]{3,2,1,0:T(8,128)(2,1)S(1)} async-done(((bf16[4,2,16,512]{3,2,1,0:T(8,128)(2,1)}), bf16[4,2,16,512]{3,2,1,0:T(8,128)(2,1)S(1)}, u32[]{:S(2)}, u32[]{:S(2)}) %all-to-all-start) | async-done | bytes 131104 | tf_op jit(solution)/shard_map/all_to_all | solution.py:14
  49.5 2.0 %convolution_add_fusion.2 = f32[8,1040,64]{1,2,0:T(8,128)} fusion(f32[8,1040,64]{1,2,0:T(8,128)S(1)} %get-tuple-element.100, f32[8,1040]{1,0:T(8,128)S(1)} %get-tuple-element.97, f32[8,1040]{1,0:T(8,128)S(1)} %broadcast_maximum_fusion, bf16[64,8,64]{2,1,0:T(8,128)(2,1)S(1)} %reshape_squeeze.7), kind=kOutput, calls=%fused_computation.19 | convolution fusion | flops 69754880 | bytes 4391936 | tf_op jit(solution)/shard_map/hnk,khd->hnd/dot_general | solution.py:107
  51.5 88.3 %while.16 = (s32[]{:T(128)}, bf16[2,64,512]{2,1,0:T(8,128)(2,1)S(1)}, f32[8,1040]{1,0:T(8,128)}, f32[8,1040]{1,0:T(8,128)}, f32[8,1040,64]{1,2,0:T(8,128)}, /*index=5*/bf16[1040,8,64]{0,2,1:T(8,128)(2,1)S(1)}, s32[]{:T(128)}) while((s32[]{:T(128)}, bf16[2,64,512]{2,1,0:T(8,128)(2,1)S(1)}, f32[8,1040]{1,0:T(8,128)}, f32[8,1040]{1,0:T(8,128)}, ...), condition=%wide.region_7.0_spmd, body=%wide.region_4.0_spmd.sunk | while | flops 140591360 | bytes 32176440 | solution.py:62
  51.5 5.3 %collective-permute-done = bf16[2,64,512]{2,1,0:T(8,128)(2,1)S(1)} collective-permute-done((bf16[2,64,512]{2,1,0:T(8,128)(2,1)S(1)}, bf16[2,64,512]{2,1,0:T(8,128)(2,1)S(1)}, u32[]{:S(2)}, u32[]{:S(2)}) %collective-permute-start) | collective-permute-done | bytes 131104 | tf_op jit(solution)/shard_map/while/body/eval_jaxpr/ppermute | solution.py:24
  61.6 1.1 convolution_add_fusion.6
  62.7 1.4 copy-done.2
  64.1 5.3 %collective-permute-done = bf16[2,64,512]{2,1,0:T(8,128)(2,1)S(1)} collective-permute-done((bf16[2,64,512]{2,1,0:T(8,128)(2,1)S(1)}, bf16[2,64,512]{2,1,0:T(8,128)(2,1)S(1)}, u32[]{:S(2)}, u32[]{:S(2)}) %collective-permute-start) | collective-permute-done | bytes 131104 | tf_op jit(solution)/shard_map/while/body/eval_jaxpr/ppermute | solution.py:24
  74.2 1.1 convolution_add_fusion.6
  75.4 1.4 copy-done.2
  76.7 5.3 %collective-permute-done = bf16[2,64,512]{2,1,0:T(8,128)(2,1)S(1)} collective-permute-done((bf16[2,64,512]{2,1,0:T(8,128)(2,1)S(1)}, bf16[2,64,512]{2,1,0:T(8,128)(2,1)S(1)}, u32[]{:S(2)}, u32[]{:S(2)}) %collective-permute-start) | collective-permute-done | bytes 131104 | tf_op jit(solution)/shard_map/while/body/eval_jaxpr/ppermute | solution.py:24
  88.0 1.4 copy-done.2
  89.3 5.3 %collective-permute-done = bf16[2,64,512]{2,1,0:T(8,128)(2,1)S(1)} collective-permute-done((bf16[2,64,512]{2,1,0:T(8,128)(2,1)S(1)}, bf16[2,64,512]{2,1,0:T(8,128)(2,1)S(1)}, u32[]{:S(2)}, u32[]{:S(2)}) %collective-permute-start) | collective-permute-done | bytes 131104 | tf_op jit(solution)/shard_map/while/body/eval_jaxpr/ppermute | solution.py:24
  100.6 1.4 copy-done.2
  102.0 5.3 %collective-permute-done = bf16[2,64,512]{2,1,0:T(8,128)(2,1)S(1)} collective-permute-done((bf16[2,64,512]{2,1,0:T(8,128)(2,1)S(1)}, bf16[2,64,512]{2,1,0:T(8,128)(2,1)S(1)}, u32[]{:S(2)}, u32[]{:S(2)}) %collective-permute-start) | collective-permute-done | bytes 131104 | tf_op jit(solution)/shard_map/while/body/eval_jaxpr/ppermute | solution.py:24
  113.2 1.4 copy-done.2
  114.6 5.3 %collective-permute-done = bf16[2,64,512]{2,1,0:T(8,128)(2,1)S(1)} collective-permute-done((bf16[2,64,512]{2,1,0:T(8,128)(2,1)S(1)}, bf16[2,64,512]{2,1,0:T(8,128)(2,1)S(1)}, u32[]{:S(2)}, u32[]{:S(2)}) %collective-permute-start) | collective-permute-done | bytes 131104 | tf_op jit(solution)/shard_map/while/body/eval_jaxpr/ppermute | solution.py:24
  125.8 1.4 copy-done.2
  127.2 5.3 %collective-permute-done = bf16[2,64,512]{2,1,0:T(8,128)(2,1)S(1)} collective-permute-done((bf16[2,64,512]{2,1,0:T(8,128)(2,1)S(1)}, bf16[2,64,512]{2,1,0:T(8,128)(2,1)S(1)}, u32[]{:S(2)}, u32[]{:S(2)}) %collective-permute-start) | collective-permute-done | bytes 131104 | tf_op jit(solution)/shard_map/while/body/eval_jaxpr/ppermute | solution.py:24
  138.4 1.4 copy-done.2
  139.8 2.0 %divide_convert_fusion = bf16[8,1040,64]{1,2,0:T(8,128)(2,1)S(1)} fusion(f32[8,1040,64]{1,2,0:T(8,128)} %get-tuple-element.35, f32[8,1040]{1,0:T(8,128)} %get-tuple-element.36), kind=kLoop, calls=%fused_computation.24 | loop fusion | flops 1064960 | bytes 3228160 | tf_op jit(solution)/shard_map/convert_element_type | solution.py:134
  143.1 1.3 copy-done.7
  144.9 8.4 %fusion.13 = bf16[1040,512]{1,0:T(8,128)(2,1)S(1)} fusion(f32[1040,512]{1,0:T(8,128)} %copy-done.7, bf16[2048,512]{1,0:T(8,128)(2,1)S(1)} %copy-done, bf16[512,2048]{1,0:T(8,128)(2,1)} %param.22, f32[1040]{0:T(1024)S(1)} %add_rsqrt_fusion, f32[1040]{0:T(1024)S(1)} %broadcast_multiply_fusion), kind=kOutput, calls=%fused_computation.22 | convolution fusion | flops 4383907840 | bytes 7397504 | tf_op jit(solution)/shard_map/dot_general | solution.py:141
  (257 shorter events, 61.0 us)
Async XLA Ops:
  0.6 144.2 %copy-start = (bf16[2048,512]{1,0:T(8,128)(2,1)S(1)}, bf16[2048,512]{1,0:T(8,128)(2,1)}, u32[]{:S(2)}) copy-start(bf16[2048,512]{1,0:T(8,128)(2,1)} %param.23) | copy-start | bytes 6291460
  23.6 3.9 %copy-start.19 = (pred[16,64]{1,0:T(8,128)(4,1)S(1)}, pred[16,64]{1,0:T(8,128)(4,1)}, u32[]{:S(2)}) copy-start(pred[16,64]{1,0:T(8,128)(4,1)} %get-tuple-element.122) | copy-start | bytes 3076
  23.6 3.9 %copy-start.20 = (pred[16,64]{1,0:T(8,128)(4,1)S(1)}, pred[16,64]{1,0:T(8,128)(4,1)}, u32[]{:S(2)}) copy-start(pred[16,64]{1,0:T(8,128)(4,1)} %get-tuple-element.123) | copy-start | bytes 3076
  23.6 3.9 %copy-start.21 = (pred[16,64]{1,0:T(8,128)(4,1)S(1)}, pred[16,64]{1,0:T(8,128)(4,1)}, u32[]{:S(2)}) copy-start(pred[16,64]{1,0:T(8,128)(4,1)} %get-tuple-element.124) | copy-start | bytes 3076
  23.6 3.9 %copy-start.22 = (pred[16,64]{1,0:T(8,128)(4,1)S(1)}, pred[16,64]{1,0:T(8,128)(4,1)}, u32[]{:S(2)}) copy-start(pred[16,64]{1,0:T(8,128)(4,1)} %get-tuple-element.125) | copy-start | bytes 3076
  23.6 3.9 %copy-start.23 = (pred[16,64]{1,0:T(8,128)(4,1)S(1)}, pred[16,64]{1,0:T(8,128)(4,1)}, u32[]{:S(2)}) copy-start(pred[16,64]{1,0:T(8,128)(4,1)} %get-tuple-element.126) | copy-start | bytes 3076
  23.6 3.9 %copy-start.24 = (pred[16,64]{1,0:T(8,128)(4,1)S(1)}, pred[16,64]{1,0:T(8,128)(4,1)}, u32[]{:S(2)}) copy-start(pred[16,64]{1,0:T(8,128)(4,1)} %get-tuple-element.127) | copy-start | bytes 3076
  23.6 3.9 %copy-start.25 = (pred[16,64]{1,0:T(8,128)(4,1)S(1)}, pred[16,64]{1,0:T(8,128)(4,1)}, u32[]{:S(2)}) copy-start(pred[16,64]{1,0:T(8,128)(4,1)} %get-tuple-element.128) | copy-start | bytes 3076
  23.6 3.9 %copy-start.26 = (pred[16,64]{1,0:T(8,128)(4,1)S(1)}, pred[16,64]{1,0:T(8,128)(4,1)}, u32[]{:S(2)}) copy-start(pred[16,64]{1,0:T(8,128)(4,1)} %get-tuple-element.129) | copy-start | bytes 3076
  23.6 3.9 %copy-start.27 = (pred[16,64]{1,0:T(8,128)(4,1)S(1)}, pred[16,64]{1,0:T(8,128)(4,1)}, u32[]{:S(2)}) copy-start(pred[16,64]{1,0:T(8,128)(4,1)} %get-tuple-element.130) | copy-start | bytes 3076
  23.7 3.9 %copy-start.28 = (pred[16,64]{1,0:T(8,128)(4,1)S(1)}, pred[16,64]{1,0:T(8,128)(4,1)}, u32[]{:S(2)}) copy-start(pred[16,64]{1,0:T(8,128)(4,1)} %get-tuple-element.131) | copy-start | bytes 3076
  23.7 3.9 %copy-start.29 = (pred[16,64]{1,0:T(8,128)(4,1)S(1)}, pred[16,64]{1,0:T(8,128)(4,1)}, u32[]{:S(2)}) copy-start(pred[16,64]{1,0:T(8,128)(4,1)} %get-tuple-element.132) | copy-start | bytes 3076
  23.7 3.9 %copy-start.30 = (pred[16,64]{1,0:T(8,128)(4,1)S(1)}, pred[16,64]{1,0:T(8,128)(4,1)}, u32[]{:S(2)}) copy-start(pred[16,64]{1,0:T(8,128)(4,1)} %get-tuple-element.133) | copy-start | bytes 3076
  23.7 3.9 %copy-start.31 = (pred[16,64]{1,0:T(8,128)(4,1)S(1)}, pred[16,64]{1,0:T(8,128)(4,1)}, u32[]{:S(2)}) copy-start(pred[16,64]{1,0:T(8,128)(4,1)} %get-tuple-element.134) | copy-start | bytes 3076
  23.7 4.0 %copy-start.32 = (f32[16]{0:T(128)S(1)}, f32[16]{0:T(128)}, u32[]{:S(2)}) copy-start(f32[16]{0:T(128)} %multiply_add_fusion.1) | copy-start | bytes 196
  27.7 3.5 %copy-start.3 = (f32[1024,512]{1,0:T(8,128)S(1)}, f32[1024,512]{1,0:T(8,128)}, u32[]{:S(2)}) copy-start(f32[1024,512]{1,0:T(8,128)} %fusion.40) | copy-start | bytes 6291460
  29.4 2.4 %copy-start.12 = (f32[16,512]{1,0:T(8,128)}, f32[16,512]{1,0:T(8,128)S(1)}, u32[]{:S(2)}) copy-start(f32[16,512]{1,0:T(8,128)S(1)} %convolution_add_fusion.4) | copy-start | bytes 98308
  33.8 12.4 %all-to-all-start = ((bf16[4,2,16,512]{3,2,1,0:T(8,128)(2,1)}), bf16[4,2,16,512]{3,2,1,0:T(8,128)(2,1)S(1)}, u32[]{:S(2)}, u32[]{:S(2)}) async-start(bf16[4,2,16,512]{3,2,1,0:T(8,128)(2,1)} %stack.19), calls=%async_computation | async-start | bytes 262144 | tf_op jit(solution)/shard_map/all_to_all | solution.py:14
  48.5 3.0 %copy-start.8 = (f32[8,1040]{1,0:T(8,128)}, f32[8,1040]{1,0:T(8,128)S(1)}, u32[]{:S(2)}) copy-start(f32[8,1040]{1,0:T(8,128)S(1)} %broadcast_maximum_fusion) | copy-start | bytes 99844
  49.5 2.0 %copy-start.18 = (bf16[4,2,16,512]{3,2,0,1:T(8,128)(2,1)S(1)}, bf16[4,2,16,512]{3,2,0,1:T(8,128)(2,1)}, u32[]{:S(2)}) copy-start(bf16[4,2,16,512]{3,2,0,1:T(8,128)(2,1)} %copy-done.17) | copy-start | bytes 393220
  51.5 5.3 %collective-permute-start = (bf16[2,64,512]{2,1,0:T(8,128)(2,1)S(1)}, bf16[2,64,512]{2,1,0:T(8,128)(2,1)S(1)}, u32[]{:S(2)}, u32[]{:S(2)}) collective-permute-start(bf16[2,64,512]{2,1,0:T(8,128)(2,1)S(1)} %get-tuple-element.192), channel_id=1, source_target_pairs={{28,0},{0,4},{4,8},{8,12},{12,16},{16,20},{20,24},{24,28},{29,1},{... | collective-permute-start | bytes 393224 | tf_op jit(solution)/shard_map/while/body/eval_jaxpr/ppermute | solution.py:24
  60.7 2.0 %copy-start.11 = (f32[8,1040]{1,0:T(8,128)}, f32[8,1040]{1,0:T(8,128)S(1)}, u32[]{:S(2)}) copy-start(f32[8,1040]{1,0:T(8,128)S(1)} %get-tuple-element.201) | copy-start | bytes 99844 | tf_op jit(solution)/shard_map/while
  64.1 5.3 %collective-permute-start = (bf16[2,64,512]{2,1,0:T(8,128)(2,1)S(1)}, bf16[2,64,512]{2,1,0:T(8,128)(2,1)S(1)}, u32[]{:S(2)}, u32[]{:S(2)}) collective-permute-start(bf16[2,64,512]{2,1,0:T(8,128)(2,1)S(1)} %get-tuple-element.192), channel_id=1, source_target_pairs={{28,0},{0,4},{4,8},{8,12},{12,16},{16,20},{20,24},{24,28},{29,1},{... | collective-permute-start | bytes 393224 | tf_op jit(solution)/shard_map/while/body/eval_jaxpr/ppermute | solution.py:24
  73.3 2.0 %copy-start.11 = (f32[8,1040]{1,0:T(8,128)}, f32[8,1040]{1,0:T(8,128)S(1)}, u32[]{:S(2)}) copy-start(f32[8,1040]{1,0:T(8,128)S(1)} %get-tuple-element.201) | copy-start | bytes 99844 | tf_op jit(solution)/shard_map/while
  76.7 5.3 %collective-permute-start = (bf16[2,64,512]{2,1,0:T(8,128)(2,1)S(1)}, bf16[2,64,512]{2,1,0:T(8,128)(2,1)S(1)}, u32[]{:S(2)}, u32[]{:S(2)}) collective-permute-start(bf16[2,64,512]{2,1,0:T(8,128)(2,1)S(1)} %get-tuple-element.192), channel_id=1, source_target_pairs={{28,0},{0,4},{4,8},{8,12},{12,16},{16,20},{20,24},{24,28},{29,1},{... | collective-permute-start | bytes 393224 | tf_op jit(solution)/shard_map/while/body/eval_jaxpr/ppermute | solution.py:24
  89.3 5.3 %collective-permute-start = (bf16[2,64,512]{2,1,0:T(8,128)(2,1)S(1)}, bf16[2,64,512]{2,1,0:T(8,128)(2,1)S(1)}, u32[]{:S(2)}, u32[]{:S(2)}) collective-permute-start(bf16[2,64,512]{2,1,0:T(8,128)(2,1)S(1)} %get-tuple-element.192), channel_id=1, source_target_pairs={{28,0},{0,4},{4,8},{8,12},{12,16},{16,20},{20,24},{24,28},{29,1},{... | collective-permute-start | bytes 393224 | tf_op jit(solution)/shard_map/while/body/eval_jaxpr/ppermute | solution.py:24
  102.0 5.3 %collective-permute-start = (bf16[2,64,512]{2,1,0:T(8,128)(2,1)S(1)}, bf16[2,64,512]{2,1,0:T(8,128)(2,1)S(1)}, u32[]{:S(2)}, u32[]{:S(2)}) collective-permute-start(bf16[2,64,512]{2,1,0:T(8,128)(2,1)S(1)} %get-tuple-element.192), channel_id=1, source_target_pairs={{28,0},{0,4},{4,8},{8,12},{12,16},{16,20},{20,24},{24,28},{29,1},{... | collective-permute-start | bytes 393224 | tf_op jit(solution)/shard_map/while/body/eval_jaxpr/ppermute | solution.py:24
  114.6 5.3 %collective-permute-start = (bf16[2,64,512]{2,1,0:T(8,128)(2,1)S(1)}, bf16[2,64,512]{2,1,0:T(8,128)(2,1)S(1)}, u32[]{:S(2)}, u32[]{:S(2)}) collective-permute-start(bf16[2,64,512]{2,1,0:T(8,128)(2,1)S(1)} %get-tuple-element.192), channel_id=1, source_target_pairs={{28,0},{0,4},{4,8},{8,12},{12,16},{16,20},{20,24},{24,28},{29,1},{... | collective-permute-start | bytes 393224 | tf_op jit(solution)/shard_map/while/body/eval_jaxpr/ppermute | solution.py:24
  127.2 5.3 %collective-permute-start = (bf16[2,64,512]{2,1,0:T(8,128)(2,1)S(1)}, bf16[2,64,512]{2,1,0:T(8,128)(2,1)S(1)}, u32[]{:S(2)}, u32[]{:S(2)}) collective-permute-start(bf16[2,64,512]{2,1,0:T(8,128)(2,1)S(1)} %get-tuple-element.192), channel_id=1, source_target_pairs={{28,0},{0,4},{4,8},{8,12},{12,16},{16,20},{20,24},{24,28},{29,1},{... | collective-permute-start | bytes 393224 | tf_op jit(solution)/shard_map/while/body/eval_jaxpr/ppermute | solution.py:24
  139.8 2.3 %copy-start.4 = (f32[1024,512]{1,0:T(8,128)S(1)}, f32[1024,512]{1,0:T(8,128)}, u32[]{:S(2)}) copy-start(f32[1024,512]{1,0:T(8,128)} %fusion.40) | copy-start | bytes 6291460
  139.8 2.3 %copy-start.13 = (f32[16,512]{1,0:T(8,128)S(1)}, f32[16,512]{1,0:T(8,128)}, u32[]{:S(2)}) copy-start(f32[16,512]{1,0:T(8,128)} %copy-done.12) | copy-start | bytes 98308
  139.8 2.4 %copy-start.14 = (bf16[512,512]{1,0:T(8,128)(2,1)S(1)}, bf16[512,512]{1,0:T(8,128)(2,1)}, u32[]{:S(2)}) copy-start(bf16[512,512]{1,0:T(8,128)(2,1)} %param.21) | copy-start | bytes 1572868
  (51 other events, 65.9 us)
